TPU v7x, 128 devices: a whole 4x4x4 slice. The times are simulated.
128 devices in a mesh: row: 16 (over y, x_lo, core), col: 8 (over x_hi, z).
Axes of the slice: x: 4 (x_hi: 2, x_lo: 2; x = x_hi * 2 + x_lo), y: 4, z: 4, core: 2. Of those that a mesh axis runs over, the one named last changes fastest.
Arguments:
- amplitudes: float32 [512, 32, 32, 32], P('col', 'row'), may hold values from -6 to 6
- integrals: float32 [1024, 16384], P('col', 'row'), may hold values from -0.1875 to 0.1875
- occ_energy: float32 [32], replicated, may hold values from -2 to -0.5
- vir_energy: float32 [512], replicated, may hold values from 0.3 to 3
Outputs:
- residual: float32 [16384, 16384], P('col', 'row')
All inputs are finite; a program needn't handle non-finite values.
Results may differ from a plain program's by a relative error of at most 0.00007.
Values sent between devices are 32-bit elements; how exact they have to be, the bound alone decides.
No kernel may reach another device: no remote copies, remote signals or barrier semaphores. Data moves between devices by JAX's collectives and lax.ppermute only.
A program may use at most 128 MiB of HBM per device.

v0:
```python
import jax
import jax.numpy as jnp
from jax import lax
from jax.sharding import PartitionSpec as P


def body(amplitudes, integrals, occ_energy, vir_energy):
    columns = integrals.shape[1]
    virtuals = amplitudes.shape[0]
    whole_w = lax.all_gather(integrals, "col", axis=0, tiled=True)
    occupied = amplitudes.shape[1] * lax.axis_size("row")
    portion = lax.all_gather(amplitudes, "row", axis=1, tiled=True)
    amount = portion.shape[1]
    flattened = portion.reshape(virtuals * amount, portion.shape[2] * portion.shape[3])
    product = jnp.dot(
        flattened, whole_w, preferred_element_type=jnp.float32, precision=lax.Precision.HIGHEST
    )
    folded = product.reshape(virtuals, amount, columns)
    summed = folded.reshape(virtuals * occupied, columns)
    height = summed.shape[0]
    gap_flat = (vir_energy[:, None] - occ_energy[None, :]).reshape(-1)
    row_gap = lax.dynamic_slice_in_dim(gap_flat, lax.axis_index("col") * height, height)
    col_gap = lax.dynamic_slice_in_dim(gap_flat, lax.axis_index("row") * columns, columns)
    return summed / (row_gap[:, None] + col_gap[None, :])


def solution(mesh):
    in_specs = (P("col", "row", None, None), P("col", "row"), P(), P())
    out_specs = P("col", "row")
    return jax.shard_map(body, mesh=mesh, in_specs=in_specs, out_specs=out_specs, check_vma=False)
```

profile of v0, /device:TPU:1, one launch (start us, length us, event | category | flops | bytes accessed | tf_op | source)
XLA Modules:
  0.0 217.1 jit_solution(794362143846984651)
XLA Ops:
  6.5 0.0 all-gather.3.cloned.1.call-start
  6.5 0.7 all-gather.3.cloned.1.call-update
  7.3 0.0 all-gather.5.cloned.1.call-start
  7.3 0.7 all-gather.5.cloned.1.call-update
  8.0 0.8 broadcast_subtract_fusion
  8.8 0.1 sub.20
  9.0 95.3 %all-gather.3.cloned.1.call-done = f32[64,32,32,32]{0,3,2,1:T(8,128)} async-done(((f32[64,2,32,32]{0,3,2,1:T(8,128)}), f32[64,32,32,32]{0,3,2,1:T(8,128)}) %all-gather.3.cloned.1.call-update) | async-done | bytes 8388624 | tf_op jit(solution)/shard_map/all_gather | solution.py:12
  104.3 30.4 %copy.6 = f32[64,32,32,32]{3,2,1,0:T(8,128)} copy(f32[64,32,32,32]{0,3,2,1:T(8,128)} %all-gather.3.cloned.1.call-done) | data formatting | bytes 16777216 | tf_op jit(solution)/shard_map/all_gather | solution.py:12
  134.7 26.3 %reshape.11 = f32[2048,1024]{1,0:T(8,128)} reshape(f32[64,32,32,32]{3,2,1,0:T(8,128)} %copy.6) | data formatting | bytes 16777216 | tf_op jit(solution)/shard_map/reshape | solution.py:14
  161.0 17.4 %all-gather.5.cloned.1.call-done = f32[1024,1024]{1,0:T(8,128)} async-done(((f32[128,1024]{1,0:T(8,128)}), f32[1024,1024]{1,0:T(8,128)}) %all-gather.5.cloned.1.call-update) | async-done | bytes 4194320 | tf_op jit(solution)/shard_map/all_gather | solution.py:10
  178.4 31.9 %add_divide_fusion = f32[2048,1024]{1,0:T(8,128)} fusion(f32[1024]{0:T(1024)S(1)} %dynamic_slice.7, f32[2048]{0:T(1024)S(1)} %dynamic_slice.6, f32[2048,1024]{1,0:T(8,128)} %reshape.11, f32[1024,1024]{1,0:T(8,128)} %all-gather.5.cloned.1.call-done), kind=kOutput, calls=%fused_computation | convolution fusion | flops 25773998080 | bytes 20983808 | tf_op jit(solution)/shard_map/dot_general | solution.py:15
  (2 shorter events, 0.0 us)
Async XLA Ops:
  6.5 97.8 %all-gather.3.cloned.1.call-start = ((), (), s32[]{:S(2)}) async-start(), calls=%async_computation | async-start | bytes 17825792 | tf_op jit(solution)/shard_map/all_gather | solution.py:12
  7.3 171.2 %all-gather.5.cloned.1.call-start = ((), (), s32[]{:S(2)}) async-start(), calls=%async_computation.1 | async-start | bytes 4718592 | tf_op jit(solution)/shard_map/all_gather | solution.py:10
Sparse Core Ops, SparseCore 0:
  9.1 95.2 all-gather.2
  106.7 71.7 all-gather.4
where the time goes:
time: 218 us; the launch traced here: 217 us
  waiting for transfers between devices  114 us (52%)
  local copies, waits for them, and re-layouts  56.8 us (26%)
  matrix products  31.9 us (15%)
  between operations  13.4 us (6%)
    all_gather x1, waiting for transfers between devices, body(): portion = lax.all_gather(amplitudes, 'row', axis=1, tiled=True)  95.3 us
    dot_general x1, matrix products, body(): jnp.dot(flattened, whole_w, preferred_element_type=jnp.float32, precision...  31.9 us
    all_gather x1, local copies, waits for them, and re-layouts, body(): portion = lax.all_gather(amplitudes, 'row', axis=1, tiled=True)  30.4 us
    reshape x1, local copies, waits for them, and re-layouts, body(): portion.reshape(virtuals * amount, portion.shape[2] * portion.shape[3])  26.3 us
    all_gather x1, waiting for transfers between devices, body(): whole_w = lax.all_gather(integrals, 'col', axis=0, tiled=True)  17.4 us
  transfers between devices with their start and end apart: 2, of which 2 were waited for; matrix products, arithmetic and copies ran while one was open for 27% of the time, Pallas kernels for 0%

commit v1 on v0

--- a/solution.py
+++ b/solution.py
@@ -9,7 +9,10 @@
     virtuals = amplitudes.shape[0]
     whole_w = lax.all_gather(integrals, "col", axis=0, tiled=True)
     occupied = amplitudes.shape[1] * lax.axis_size("row")
-    portion = lax.all_gather(amplitudes, "row", axis=1, tiled=True)
+    size = lax.axis_size("row")
+    blocks = jnp.stack([amplitudes for _ in range(size)])
+    blocks = lax.all_to_all(blocks, "row", split_axis=0, concat_axis=0)
+    portion = jnp.concatenate(blocks, axis=1)
     amount = portion.shape[1]
     flattened = portion.reshape(virtuals * amount, portion.shape[2] * portion.shape[3])
     product = jnp.dot(

time: 218 us -> 316 us (1.45)
  local copies, waits for them, and re-layouts: 56.8 us -> 114 us
  other arithmetic: 0.83 us -> 25.4 us
  waiting for transfers between devices: 114 us -> 122 us
  starting transfers between devices: 0.04 us -> 7.08 us
    all_to_all x0 -> x1, waiting for transfers between devices: none -> 122 us  [body(): blocks = lax.all_to_all(blocks, 'row', split_axis=0, concat_axis=0)]
    all_gather x1 -> x0, waiting for transfers between devices: 95.3 us -> none  [body(): portion = lax.all_gather(amplitudes, 'row', axis=1, tiled=True)]
    unnamed x0 -> x13, local copies, waits for them, and re-layouts: none -> 44.9 us
    all_gather x1 -> x0, local copies, waits for them, and re-layouts: 30.4 us -> none  [body(): portion = lax.all_gather(amplitudes, 'row', axis=1, tiled=True)]
    another operation x0 -> x1, local copies, waits for them, and re-layouts: none -> 26.1 us  [body(): portion.reshape(virtuals * amount, portion.shape[2] * portion.shape[3])]
    all_to_all x0 -> x1, other arithmetic: none -> 25.2 us  [body(): blocks = lax.all_to_all(blocks, 'row', split_axis=0, concat_axis=0)]
    all_gather x1, waiting for transfers between devices: 17.4 us -> 0.01 us  [body(): whole_w = lax.all_gather(integrals, 'col', axis=0, tiled=True)]
    reshape x1 -> x2, local copies, waits for them, and re-layouts: 26.3 us -> 41.9 us  [body(): portion = jnp.concatenate(blocks, axis=1)]
  transfers between devices with their start and end apart: 2 -> 2, of which waited for: 2 -> 1; matrix products, arithmetic and copies ran while one was open for 27% -> 35% of each run, Pallas kernels for 0% -> 0%
where the time goes in v1:
time: 316 us; the launch traced here: 314 us
  waiting for transfers between devices  122 us (39%)
  local copies, waits for them, and re-layouts  114 us (36%)
  matrix products  32.1 us (10%)
  other arithmetic  25.4 us (8%)
  between operations  13.5 us (4%)
  starting transfers between devices  7.08 us (2%)
    all_to_all x1, waiting for transfers between devices, body(): blocks = lax.all_to_all(blocks, 'row', split_axis=0, concat_axis=0)  122 us
    unnamed x13, local copies, waits for them, and re-layouts  44.9 us
    reshape x2, local copies, waits for them, and re-layouts, body(): portion = jnp.concatenate(blocks, axis=1)  41.9 us
    dot_general x1, matrix products, body(): jnp.dot(flattened, whole_w, preferred_element_type=jnp.float32, precision...  32.1 us
    another operation x1, local copies, waits for them, and re-layouts, body(): portion.reshape(virtuals * amount, portion.shape[2] * portion.shape[3])  26.1 us
    all_to_all x1, other arithmetic, body(): blocks = lax.all_to_all(blocks, 'row', split_axis=0, concat_axis=0)  25.2 us
    all_to_all x1, starting transfers between devices, body(): blocks = lax.all_to_all(blocks, 'row', split_axis=0, concat_axis=0)  7.05 us
  transfers between devices with their start and end apart: 2, of which 1 were waited for; matrix products, arithmetic and copies ran while one was open for 35% of the time, Pallas kernels for 0%

profile of v1, /device:TPU:1, one launch (start us, length us, event | category | flops | bytes accessed | tf_op | source)
XLA Modules:
  0.0 314.0 jit_solution(1659576743852906545)
XLA Ops:
  6.5 0.0 copy-start
  6.5 1.2 copy-done
  7.8 7.9 %broadcast_bitcast_fusion = f32[16,2,32,32,64]{4,3,2,1,0:T(8,128)} fusion(f32[64,2,32,32]{0,3,2,1:T(8,128)S(1)} %copy-done), kind=kLoop, calls=%fused_computation.3 | loop fusion | bytes 8912896
  15.7 18.4 %reshape.14 = f32[16,1,131072]{2,1,0:T(1,128)} reshape(f32[16,2,32,32,64]{4,3,2,1,0:T(8,128)} %broadcast_bitcast_fusion) | data formatting | bytes 16777216
  34.1 0.0 copy-start.3
  34.1 0.0 copy-start.4
  34.1 7.0 %all-to-all-start = ((f32[16,1,131072]{2,1,0:T(1,128)}), f32[16,1,131072]{2,1,0:T(1,128)}, u32[]{:S(2)}, u32[]{:S(2)}) async-start(f32[16,1,131072]{2,1,0:T(1,128)} %reshape.14), calls=%async_computation | async-start | bytes 16777216 | tf_op jit(solution)/shard_map/all_to_all | solution.py:14
  41.1 0.0 all-gather.2.cloned.1.call-start
  41.2 0.7 all-gather.2.cloned.1.call-update
  41.9 0.0 copy-done.3
  41.9 0.0 copy-done.4
  41.9 0.1 broadcast_subtract_fusion
  42.0 0.1 sub.20
  42.1 0.0 copy-start.2
  42.2 121.7 %all-to-all-done = f32[16,1,131072]{2,1,0:T(1,128)} async-done(((f32[16,1,131072]{2,1,0:T(1,128)}), f32[16,1,131072]{2,1,0:T(1,128)}, u32[]{:S(2)}, u32[]{:S(2)}) %all-to-all-start) | async-done | bytes 8388640 | tf_op jit(solution)/shard_map/all_to_all | solution.py:14
  163.8 0.5 broadcast.8
  164.3 25.2 %reduce = f32[16,131072]{1,0:T(8,128)} reduce(f32[16,1,131072]{2,1,0:T(1,128)} %all-to-all-done, f32[]{:T(128)} %broadcast.8), dimensions={1}, to_apply=%all_to_all.3.reduce_sub_computation | reduce | bytes 16777220 | tf_op jit(solution)/shard_map/all_to_all | solution.py:14
  189.6 0.0 copy-done.2
  189.6 17.4 %reshape.15 = f32[16,2,32,32,64]{4,3,2,1,0:T(8,128)} reshape(f32[16,131072]{1,0:T(8,128)} %reduce) | data formatting | bytes 16777216
  206.9 11.6 %bitcast_bitcast_fusion = f32[64,16,2,32,32]{0,4,3,2,1:T(8,128)} fusion(f32[16,2,32,32,64]{4,3,2,1,0:T(8,128)} %reshape.15), kind=kLoop, calls=%fused_computation.2 | loop fusion | bytes 16777216 | tf_op jit(solution)/shard_map/reshape | solution.py:15
  218.5 30.4 %copy.7 = f32[64,16,2,32,32]{4,3,2,1,0:T(8,128)} copy(f32[64,16,2,32,32]{0,4,3,2,1:T(8,128)} %bitcast_bitcast_fusion) | data formatting | bytes 16777216 | tf_op jit(solution)/shard_map/reshape | solution.py:15
  248.9 0.0 dynamic-slice-start
  248.9 0.0 dynamic-slice-start.1
  248.9 26.1 %reshape_reshape.3 = f32[2048,1024]{1,0:T(8,128)} reshape(f32[64,16,2,32,32]{4,3,2,1,0:T(8,128)} %copy.7) | data formatting | bytes 16777216 | tf_op jit(solution)/shard_map/reshape;reshape | solution.py:17
  274.9 0.0 all-gather.2.cloned.1.call-done
  274.9 0.0 dynamic-slice-done
  274.9 0.0 dynamic-slice-done.1
  275.0 0.0 copy-start.1
  275.0 32.1 %add_divide_fusion = f32[2048,1024]{1,0:T(8,128)} fusion(f32[1024]{0:T(1024)S(1)} %dynamic-slice-done.1, f32[2048]{0:T(1024)S(1)} %dynamic-slice-done, f32[2048,1024]{1,0:T(8,128)} %reshape_reshape.3, f32[1024,1024]{1,0:T(8,128)} %all-gather.2.cloned.1.call-done), kind=kOutput, calls=%fused_computation | convolution fusion | flops 25773998080 | bytes 20983808 | tf_op jit(solution)/shard_map/dot_general | solution.py:18
  307.1 0.0 copy-done.1
Async XLA Ops:
  6.5 1.2 copy-start
  34.1 7.8 %copy-start.3 = (f32[512]{0:T(512)S(1)}, f32[512]{0:T(512)}, u32[]{:S(2)}) copy-start(f32[512]{0:T(512)} %param.7) | copy-start | bytes 6148
  34.1 7.8 %copy-start.4 = (f32[32]{0:T(128)S(1)}, f32[32]{0:T(128)}, u32[]{:S(2)}) copy-start(f32[32]{0:T(128)} %param.6) | copy-start | bytes 388
  34.1 129.7 %all-to-all-start = ((f32[16,1,131072]{2,1,0:T(1,128)}), f32[16,1,131072]{2,1,0:T(1,128)}, u32[]{:S(2)}, u32[]{:S(2)}) async-start(f32[16,1,131072]{2,1,0:T(1,128)} %reshape.14), calls=%async_computation | async-start | bytes 16777216 | tf_op jit(solution)/shard_map/all_to_all | solution.py:14
  41.1 233.8 %all-gather.2.cloned.1.call-start = ((), (), s32[]{:S(2)}) async-start(), calls=%async_computation.1 | async-start | bytes 4718592 | tf_op jit(solution)/shard_map/all_gather | solution.py:10
  42.1 147.4 %copy-start.2 = (f32[16384]{0:T(1024)}, f32[16384]{0:T(1024)S(1)}, u32[]{:S(2)}) copy-start(f32[16384]{0:T(1024)S(1)} %sub.20) | copy-start | bytes 196612
  248.9 26.1 %dynamic-slice-start = ((f32[16384]{0:T(1024)}, s32[]{:T(128)}), f32[2048]{0:T(1024)S(1)}, s32[]{:S(2)}) async-start(f32[16384]{0:T(1024)} %copy-done.2, s32[]{:T(128)} %select_n.6), calls=%async_computation.2 | async-start | bytes 16896 | tf_op jit(solution)/shard_map/dynamic_slice | solution.py:25
  248.9 26.1 %dynamic-slice-start.1 = ((f32[16384]{0:T(1024)}, s32[]{:T(128)}), f32[1024]{0:T(1024)S(1)}, s32[]{:S(2)}) async-start(f32[16384]{0:T(1024)} %copy-done.2, s32[]{:T(128)} %select_n.7), calls=%async_computation.3 | async-start | bytes 8704 | tf_op jit(solution)/shard_map/dynamic_slice | solution.py:26
  275.0 32.2 %copy-start.1 = (f32[64,2,32,32]{0,3,2,1:T(8,128)S(1)}, f32[64,2,32,32]{0,3,2,1:T(8,128)}, u32[]{:S(2)}) copy-start(f32[64,2,32,32]{0,3,2,1:T(8,128)} %param.4) | copy-start | bytes 1572868
Sparse Core Ops, SparseCore 0:
  44.3 101.6 all-gather.1
